TPU v7x, 32 devices: a whole 2x2x4 slice. The times are simulated.
32 devices in a mesh: tile: 8 (over z, x), wave: 4 (over y, core).
Axes of the slice: x: 2, y: 2, z: 4, core: 2. Of those that a mesh axis runs over, the one named last changes fastest.
Arguments:
- fibre_data: bfloat16 [128, 256, 128], P('wave', 'tile'), may hold values from -162 to 162
- kernels: bfloat16 [4, 256, 4, 128, 128], P('wave', 'tile'), may hold values from -0.25 to 0.25
- block_index: int32 [4, 256, 4], P('wave', 'tile'), may hold values from 0 to 127, as said below
- live_count: int32 [8], P('tile'), may hold values from 8 to 32, as said below
Outputs:
- solution: float32 [128, 128, 128], P('wave', 'tile')
- residual: float32 [128, 128, 128], P('wave', 'tile')
Inputs may be any that keep to these rules, and one draw needn't show every extreme that they name: `block_index`: A group of tile t (groups t * 32 to (t + 1) * 32 - 1) names only blocks from max(t * 16 - 4, 0) to min((t + 1) * 16 + 4, 128) - 1; for every kernel set and tile, some live group of that tile names both ends of that range. `live_count`: some tile has all 32 groups live.
All inputs are finite; a program needn't handle non-finite values.
Results may differ from a plain program's by a relative error of at most 0.035.
Values may be sent and summed in bfloat16 or wider, within the bound.
No kernel may reach another device: no remote copies, remote signals or barrier semaphores. Data moves between devices by JAX's collectives and lax.ppermute only.
A program may use at most 64 MiB of HBM per device.

v0:
```python
import jax
import jax.numpy as jnp
from jax import lax
from jax.sharding import PartitionSpec as P

HALO_BLOCKS = 4
BLOCKS_DEV = 16
ITERATIONS = 3
TIKHONOV = 0.5


def from_behind(value, axis, by):
    size = lax.axis_size(axis)
    pairs = [(i, i + by) for i in range(size) if 0 <= i + by < size]
    return lax.ppermute(value, axis, pairs)


def extended(value, sides, width):
    for axis, dim in sides:
        size, length = (lax.axis_size(axis), value.shape[dim])
        up = [(i, (i + 1) % size) for i in range(size - 1)]
        down = [(j, i) for i, j in up]
        last = lax.slice_in_dim(value, length - width, length, axis=dim)
        initial = lax.slice_in_dim(value, 0, width, axis=dim)
        before = lax.ppermute(last, axis, up)
        after = lax.ppermute(initial, axis, down)
        value = jnp.concatenate([before, value, after], axis=dim)
    return value


def select_table(local_index, extent):
    return (local_index[..., None] == jnp.arange(extent, dtype=jnp.int32)).astype(jnp.bfloat16)


def forward_image(window16, kernels, selector16, live_mask):
    kernel_sets = kernels.shape[0]
    shaped = window16.reshape(
        kernel_sets, window16.shape[0] // kernel_sets, window16.shape[1], window16.shape[2]
    )
    picked = jnp.einsum(
        "cgrb,cwbs->cwgrs", selector16, shaped, preferred_element_type=jnp.float32
    ).astype(jnp.bfloat16)
    applied = jnp.einsum("cwgrs,cgrsf->cwgf", picked, kernels, preferred_element_type=jnp.float32)
    return (applied * live_mask[None, None, :, None]).astype(jnp.bfloat16)


def adjoint_image(image16, kernels, selector16):
    spread = jnp.einsum("cwgf,cgrsf->cwgrs", image16, kernels, preferred_element_type=jnp.float32)
    upper_part = spread.astype(jnp.bfloat16)
    lower_part = (spread - upper_part.astype(jnp.float32)).astype(jnp.bfloat16)
    summed = jnp.einsum(
        "cgrb,cwgrs->cwbs", selector16, upper_part, preferred_element_type=jnp.float32
    )
    summed = summed + jnp.einsum(
        "cgrb,cwgrs->cwbs", selector16, lower_part, preferred_element_type=jnp.float32
    )
    return summed.reshape(summed.shape[0] * summed.shape[1], summed.shape[2], summed.shape[3])


def shards(fibre_data, kernels, block_index, live_count):
    extent = BLOCKS_DEV + 2 * HALO_BLOCKS
    first_block = lax.axis_index("tile") * BLOCKS_DEV - HALO_BLOCKS
    selector16 = select_table(block_index - first_block, extent)
    groups = block_index.shape[1]
    live_mask = (jnp.arange(groups, dtype=jnp.int32) < live_count[0]).astype(jnp.float32)
    kernel_sets = kernels.shape[0]
    observed = fibre_data * live_mask.astype(jnp.bfloat16)[None, :, None]
    observed = observed.reshape(
        kernel_sets, fibre_data.shape[0] // kernel_sets, groups, fibre_data.shape[2]
    )
    partial_rhs = adjoint_image(observed, kernels, selector16)
    rim_width = HALO_BLOCKS

    def settle(partial_value):
        owned_part = partial_value[:, rim_width : rim_width + BLOCKS_DEV]
        from_right = from_behind(
            partial_value[:, :rim_width].astype(jnp.bfloat16), "tile", -1
        ).astype(jnp.float32)
        from_left = from_behind(
            partial_value[:, BLOCKS_DEV + rim_width :].astype(jnp.bfloat16), "tile", 1
        ).astype(jnp.float32)
        owned_part = owned_part.at[:, :rim_width].add(from_left)
        return owned_part.at[:, BLOCKS_DEV - rim_width :].add(from_right)

    def operate(vector):
        padded = extended(vector.astype(jnp.bfloat16), (("tile", 1),), HALO_BLOCKS)
        image16 = forward_image(padded, kernels, selector16, live_mask)
        return settle(adjoint_image(image16, kernels, selector16)) + TIKHONOV * vector

    def local_inner(first_vector, second_vector):
        return jnp.sum(first_vector * second_vector)

    rhs = settle(partial_rhs)
    solution = jnp.zeros_like(rhs)
    residual = rhs

    def paired(vector, applied):
        return lax.psum(
            (local_inner(vector, vector), local_inner(vector, applied)), ("tile", "wave")
        )

    applied = operate(residual)
    current, product = paired(residual, applied)
    step_size = current / product
    direction = residual
    applied_dir = applied
    for iteration in range(ITERATIONS):
        solution = solution + step_size * direction
        residual = residual - step_size * applied_dir
        if iteration + 1 < ITERATIONS:
            applied = operate(residual)
            following, product = paired(residual, applied)
            beta_ratio = following / current
            step_size = following / (product - beta_ratio * following / step_size)
            direction = residual + beta_ratio * direction
            applied_dir = applied + beta_ratio * applied_dir
            current = following
    return (solution, residual)


def solution(mesh):
    in_specs = (
        P("wave", "tile", None),
        P("wave", "tile", None, None, None),
        P("wave", "tile", None),
        P("tile"),
    )
    out_specs = (P("wave", "tile", None), P("wave", "tile", None))
    return jax.shard_map(shards, mesh=mesh, in_specs=in_specs, out_specs=out_specs, check_vma=False)
```

profile of v0, /device:TPU:0, one launch (start us, length us, event | category | flops | bytes accessed | tf_op | source)
XLA Modules:
  0.0 242.5 jit_solution(4463199943497567733)
XLA Ops:
  1.3 1.0 multiply_bitcast_fusion
  2.3 3.7 %fusion.12 = f32[32,32,4,128]{3,1,2,0:T(8,128)S(1)} fusion(bf16[1,32,4,128,128]{4,3,2,1,0:T(8,128)(2,1)} %param.21, bf16[32,32,128,1]{2,1,0,3:T(8,128)(2,1)S(1)} %multiply_bitcast_fusion), kind=kOutput, calls=%fused_computation.12 | convolution fusion | flops 134217728 | bytes 6553600 | tf_op jit(solution)/shard_map/cwgf,cgrsf->cwgrs/dot_general | solution.py:48
  6.1 0.3 fusion.71
  6.6 0.4 copy-done.4
  7.0 0.7 convolution_bitcast_fusion.6
  7.7 0.7 fusion.153
  8.4 4.9 %collective-permute-start = (bf16[32,4,128]{2,1,0:T(4,128)(2,1)S(1)}, bf16[32,4,128]{2,1,0:T(4,128)(2,1)S(1)}, u32[]{:S(2)}, u32[]{:S(2)}) collective-permute-start(bf16[32,4,128]{2,1,0:T(4,128)(2,1)S(1)} %get-tuple-element.124), channel_id=1, source_target_pairs={{0,4},{4,8},{8,12},{12,16},{16,20},{20,24},{24,28},{1,5},{5,9},{9,... | collective-permute-start | bytes 98312 | tf_op jit(solution)/shard_map/ppermute | solution.py:15
  13.3 1.3 collective-permute-start.1
  14.9 4.2 %collective-permute-done.1 = bf16[32,4,128]{2,1,0:T(4,128)(2,1)S(1)} collective-permute-done((bf16[32,4,128]{2,1,0:T(4,128)(2,1)S(1)}, bf16[32,4,128]{2,1,0:T(4,128)(2,1)S(1)}, u32[]{:S(2)}, u32[]{:S(2)}) %collective-permute-start.1) | collective-permute-done | bytes 32800 | tf_op jit(solution)/shard_map/ppermute | solution.py:15
  19.2 1.3 collective-permute-start.3
  20.5 5.0 %collective-permute-start.2 = (bf16[32,4,128]{2,1,0:T(4,128)(2,1)S(1)}, bf16[32,4,128]{2,1,0:T(4,128)(2,1)S(1)}, u32[]{:S(2)}, u32[]{:S(2)}) collective-permute-start(bf16[32,4,128]{2,1,0:T(4,128)(2,1)S(1)} %get-tuple-element.129), channel_id=1, source_target_pairs={{0,4},{4,8},{8,12},{12,16},{16,20},{20,24},{24,28},{1,5},{5,9},{9,... | collective-permute-start | bytes 98312 | tf_op jit(solution)/shard_map/ppermute | solution.py:25
  25.6 1.6 collective-permute-done.2
  27.1 0.5 fusion.18
  27.6 6.0 %fusion.8 = f32[32,32,4,128]{3,1,2,0:T(8,128)S(1)} fusion(bf16[1,32,4,128,128]{4,3,2,1,0:T(8,128)(2,1)} %param.21, bf16[32,32,4,128]{3,1,2,0:T(8,128)(2,1)S(1)} %fusion.18, f32[32]{0:T(128)S(1)} %compare_convert_fusion), kind=kOutput, calls=%fused_computation.8 | convolution fusion | flops 268697600 | bytes 7340160 | tf_op jit(solution)/shard_map/cwgf,cgrsf->cwgrs/dot_general | solution.py:48
  33.6 0.3 fusion.72
  34.2 0.7 convolution_bitcast_fusion.4
  34.8 0.7 fusion.154
  35.6 4.8 %collective-permute-start.4 = (bf16[32,4,128]{2,1,0:T(4,128)(2,1)S(1)}, bf16[32,4,128]{2,1,0:T(4,128)(2,1)S(1)}, u32[]{:S(2)}, u32[]{:S(2)}) collective-permute-start(bf16[32,4,128]{2,1,0:T(4,128)(2,1)S(1)} %get-tuple-element.122), channel_id=1, source_target_pairs={{0,4},{4,8},{8,12},{12,16},{16,20},{20,24},{24,28},{1,5},{5,9},{9,... | collective-permute-start | bytes 98312 | tf_op jit(solution)/shard_map/ppermute | solution.py:15
  40.4 1.3 collective-permute-start.5
  42.0 5.4 %collective-permute-done.5 = bf16[32,4,128]{2,1,0:T(4,128)(2,1)S(1)} collective-permute-done((bf16[32,4,128]{2,1,0:T(4,128)(2,1)S(1)}, bf16[32,4,128]{2,1,0:T(4,128)(2,1)S(1)}, u32[]{:S(2)}, u32[]{:S(2)}) %collective-permute-start.5) | collective-permute-done | bytes 32800 | tf_op jit(solution)/shard_map/ppermute | solution.py:15
  47.5 0.7 multiply_reduce_fusion.4
  48.2 42.1 %all-reduce.2 = (f32[]{:T(128)}, f32[]{:T(128)}) all-reduce(f32[]{:T(128)} %get-tuple-element.103, f32[]{:T(128)} %get-tuple-element.102), channel_id=1, replica_groups=mesh['tile'=8,'wave'=4] {'tile','wave'}, use_global_device_ids=true, to_apply=%region_1.0 | all-reduce | flops 2 | bytes 16 | tf_op jit(solution)/shard_map/psum | solution.py:98
  91.7 1.3 collective-permute-start.7
  93.0 5.0 %collective-permute-start.6 = (bf16[32,4,128]{2,1,0:T(4,128)(2,1)S(1)}, bf16[32,4,128]{2,1,0:T(4,128)(2,1)S(1)}, u32[]{:S(2)}, u32[]{:S(2)}) collective-permute-start(bf16[32,4,128]{2,1,0:T(4,128)(2,1)S(1)} %get-tuple-element.127), channel_id=1, source_target_pairs={{0,4},{4,8},{8,12},{12,16},{16,20},{20,24},{24,28},{1,5},{5,9},{9,... | collective-permute-start | bytes 98312 | tf_op jit(solution)/shard_map/ppermute | solution.py:25
  98.0 1.4 collective-permute-done.6
  99.4 1.5 fusion.19
  100.8 6.3 %fusion.4 = f32[32,32,4,128]{3,1,2,0:T(8,128)S(1)} fusion(bf16[1,32,4,128,128]{4,3,2,1,0:T(8,128)(2,1)} %param.21, bf16[32,32,4,128]{3,1,2,0:T(8,128)(2,1)} %fusion.19, f32[32]{0:T(128)S(1)} %compare_convert_fusion), kind=kOutput, calls=%fused_computation.4 | convolution fusion | flops 268697600 | bytes 7340160 | tf_op jit(solution)/shard_map/cwgf,cgrsf->cwgrs/dot_general | solution.py:48
  107.7 0.7 convolution_bitcast_fusion.2
  108.4 0.7 fusion.155
  109.1 4.8 %collective-permute-start.8 = (bf16[32,4,128]{2,1,0:T(4,128)(2,1)S(1)}, bf16[32,4,128]{2,1,0:T(4,128)(2,1)S(1)}, u32[]{:S(2)}, u32[]{:S(2)}) collective-permute-start(bf16[32,4,128]{2,1,0:T(4,128)(2,1)S(1)} %get-tuple-element.120), channel_id=1, source_target_pairs={{0,4},{4,8},{8,12},{12,16},{16,20},{20,24},{24,28},{1,5},{5,9},{9,... | collective-permute-start | bytes 98312 | tf_op jit(solution)/shard_map/ppermute | solution.py:15
  113.9 1.3 collective-permute-start.9
  115.5 5.4 %collective-permute-done.9 = bf16[32,4,128]{2,1,0:T(4,128)(2,1)S(1)} collective-permute-done((bf16[32,4,128]{2,1,0:T(4,128)(2,1)S(1)}, bf16[32,4,128]{2,1,0:T(4,128)(2,1)S(1)}, u32[]{:S(2)}, u32[]{:S(2)}) %collective-permute-start.9) | collective-permute-done | bytes 32800 | tf_op jit(solution)/shard_map/ppermute | solution.py:15
  121.0 0.7 multiply_reduce_fusion.2
  121.7 39.7 %all-reduce.1 = (f32[]{:T(128)}, f32[]{:T(128)}) all-reduce(f32[]{:T(128)} %get-tuple-element.101, f32[]{:T(128)} %get-tuple-element.100), channel_id=1, replica_groups=mesh['tile'=8,'wave'=4] {'tile','wave'}, use_global_device_ids=true, to_apply=%region_5.0 | all-reduce | flops 2 | bytes 16 | tf_op jit(solution)/shard_map/psum | solution.py:98
  166.0 0.9 fusion.144
  166.9 1.3 collective-permute-start.11
  168.2 4.8 %collective-permute-start.10 = (bf16[32,4,128]{2,1,0:T(4,128)(2,1)S(1)}, bf16[32,4,128]{2,1,0:T(4,128)(2,1)S(1)}, u32[]{:S(2)}, u32[]{:S(2)}) collective-permute-start(bf16[32,4,128]{2,1,0:T(4,128)(2,1)S(1)} %get-tuple-element.125), channel_id=1, source_target_pairs={{0,4},{4,8},{8,12},{12,16},{16,20},{20,24},{24,28},{1,5},{5,9},{9,... | collective-permute-start | bytes 98312 | tf_op jit(solution)/shard_map/ppermute | solution.py:25
  173.0 1.6 collective-permute-done.10
  174.6 0.5 fusion.20
  175.1 6.0 %fusion = f32[32,32,4,128]{3,1,2,0:T(8,128)S(1)} fusion(bf16[1,32,4,128,128]{4,3,2,1,0:T(8,128)(2,1)} %param.21, bf16[32,32,4,128]{3,1,2,0:T(8,128)(2,1)S(1)} %fusion.20, f32[32]{0:T(128)S(1)} %compare_convert_fusion), kind=kOutput, calls=%fused_computation | convolution fusion | flops 268697600 | bytes 7340160 | tf_op jit(solution)/shard_map/cwgf,cgrsf->cwgrs/dot_general | solution.py:48
  181.7 0.7 convolution_bitcast_fusion
  182.4 0.7 fusion.156
  183.1 4.8 %collective-permute-start.12 = (bf16[32,4,128]{2,1,0:T(4,128)(2,1)S(1)}, bf16[32,4,128]{2,1,0:T(4,128)(2,1)S(1)}, u32[]{:S(2)}, u32[]{:S(2)}) collective-permute-start(bf16[32,4,128]{2,1,0:T(4,128)(2,1)S(1)} %get-tuple-element.118), channel_id=1, source_target_pairs={{0,4},{4,8},{8,12},{12,16},{16,20},{20,24},{24,28},{1,5},{5,9},{9,... | collective-permute-start | bytes 98312 | tf_op jit(solution)/shard_map/ppermute | solution.py:15
  187.9 1.3 collective-permute-start.13
  189.5 5.4 %collective-permute-done.13 = bf16[32,4,128]{2,1,0:T(4,128)(2,1)S(1)} collective-permute-done((bf16[32,4,128]{2,1,0:T(4,128)(2,1)S(1)}, bf16[32,4,128]{2,1,0:T(4,128)(2,1)S(1)}, u32[]{:S(2)}, u32[]{:S(2)}) %collective-permute-start.13) | collective-permute-done | bytes 32800 | tf_op jit(solution)/shard_map/ppermute | solution.py:15
  195.0 0.7 multiply_reduce_fusion
  195.7 42.1 %all-reduce = (f32[]{:T(128)}, f32[]{:T(128)}) all-reduce(f32[]{:T(128)} %get-tuple-element.99, f32[]{:T(128)} %get-tuple-element.98), channel_id=1, replica_groups=mesh['tile'=8,'wave'=4] {'tile','wave'}, use_global_device_ids=true, to_apply=%region_9.0 | all-reduce | flops 2 | bytes 16 | tf_op jit(solution)/shard_map/psum | solution.py:98
  241.6 0.9 multiply_subtract_fusion
  (46 shorter events, 3.2 us)
Async XLA Ops:
  6.4 0.7 copy-start.4
  8.4 6.5 %collective-permute-start = (bf16[32,4,128]{2,1,0:T(4,128)(2,1)S(1)}, bf16[32,4,128]{2,1,0:T(4,128)(2,1)S(1)}, u32[]{:S(2)}, u32[]{:S(2)}) collective-permute-start(bf16[32,4,128]{2,1,0:T(4,128)(2,1)S(1)} %get-tuple-element.124), channel_id=1, source_target_pairs={{0,4},{4,8},{8,12},{12,16},{16,20},{20,24},{24,28},{1,5},{5,9},{9,... | collective-permute-start | bytes 98312 | tf_op jit(solution)/shard_map/ppermute | solution.py:15
  13.3 5.8 %collective-permute-start.1 = (bf16[32,4,128]{2,1,0:T(4,128)(2,1)S(1)}, bf16[32,4,128]{2,1,0:T(4,128)(2,1)S(1)}, u32[]{:S(2)}, u32[]{:S(2)}) collective-permute-start(bf16[32,4,128]{2,1,0:T(4,128)(2,1)S(1)} %get-tuple-element.123), channel_id=1, source_target_pairs={{4,0},{8,4},{12,8},{16,12},{20,16},{24,20},{28,24},{5,1},{9,5},{13... | collective-permute-start | bytes 98312 | tf_op jit(solution)/shard_map/ppermute | solution.py:15
  19.2 6.3 %collective-permute-start.3 = (bf16[32,4,128]{2,1,0:T(4,128)(2,1)S(1)}, bf16[32,4,128]{2,1,0:T(4,128)(2,1)S(1)}, u32[]{:S(2)}, u32[]{:S(2)}) collective-permute-start(bf16[32,4,128]{2,1,0:T(4,128)(2,1)S(1)} %get-tuple-element.130), channel_id=1, source_target_pairs={{4,0},{8,4},{12,8},{16,12},{20,16},{24,20},{28,24},{5,1},{9,5},{13... | collective-permute-start | bytes 98312 | tf_op jit(solution)/shard_map/ppermute | solution.py:26
  20.5 6.6 %collective-permute-start.2 = (bf16[32,4,128]{2,1,0:T(4,128)(2,1)S(1)}, bf16[32,4,128]{2,1,0:T(4,128)(2,1)S(1)}, u32[]{:S(2)}, u32[]{:S(2)}) collective-permute-start(bf16[32,4,128]{2,1,0:T(4,128)(2,1)S(1)} %get-tuple-element.129), channel_id=1, source_target_pairs={{0,4},{4,8},{8,12},{12,16},{16,20},{20,24},{24,28},{1,5},{5,9},{9,... | collective-permute-start | bytes 98312 | tf_op jit(solution)/shard_map/ppermute | solution.py:25
  35.6 6.4 %collective-permute-start.4 = (bf16[32,4,128]{2,1,0:T(4,128)(2,1)S(1)}, bf16[32,4,128]{2,1,0:T(4,128)(2,1)S(1)}, u32[]{:S(2)}, u32[]{:S(2)}) collective-permute-start(bf16[32,4,128]{2,1,0:T(4,128)(2,1)S(1)} %get-tuple-element.122), channel_id=1, source_target_pairs={{0,4},{4,8},{8,12},{12,16},{16,20},{20,24},{24,28},{1,5},{5,9},{9,... | collective-permute-start | bytes 98312 | tf_op jit(solution)/shard_map/ppermute | solution.py:15
  40.4 7.0 %collective-permute-start.5 = (bf16[32,4,128]{2,1,0:T(4,128)(2,1)S(1)}, bf16[32,4,128]{2,1,0:T(4,128)(2,1)S(1)}, u32[]{:S(2)}, u32[]{:S(2)}) collective-permute-start(bf16[32,4,128]{2,1,0:T(4,128)(2,1)S(1)} %get-tuple-element.121), channel_id=1, source_target_pairs={{4,0},{8,4},{12,8},{16,12},{20,16},{24,20},{28,24},{5,1},{9,5},{13... | collective-permute-start | bytes 98312 | tf_op jit(solution)/shard_map/ppermute | solution.py:15
  91.7 74.3 %copy-start = (f32[32,16,128]{2,1,0:T(8,128)}, f32[32,16,128]{2,1,0:T(8,128)S(1)}, u32[]{:S(2)}) copy-start(f32[32,16,128]{2,1,0:T(8,128)S(1)} %get-tuple-element.114) | copy-start | bytes 786436
  91.7 6.3 %collective-permute-start.7 = (bf16[32,4,128]{2,1,0:T(4,128)(2,1)S(1)}, bf16[32,4,128]{2,1,0:T(4,128)(2,1)S(1)}, u32[]{:S(2)}, u32[]{:S(2)}) collective-permute-start(bf16[32,4,128]{2,1,0:T(4,128)(2,1)S(1)} %get-tuple-element.128), channel_id=1, source_target_pairs={{4,0},{8,4},{12,8},{16,12},{20,16},{24,20},{28,24},{5,1},{9,5},{13... | collective-permute-start | bytes 98312 | tf_op jit(solution)/shard_map/ppermute | solution.py:26
  93.0 6.4 %collective-permute-start.6 = (bf16[32,4,128]{2,1,0:T(4,128)(2,1)S(1)}, bf16[32,4,128]{2,1,0:T(4,128)(2,1)S(1)}, u32[]{:S(2)}, u32[]{:S(2)}) collective-permute-start(bf16[32,4,128]{2,1,0:T(4,128)(2,1)S(1)} %get-tuple-element.127), channel_id=1, source_target_pairs={{0,4},{4,8},{8,12},{12,16},{16,20},{20,24},{24,28},{1,5},{5,9},{9,... | collective-permute-start | bytes 98312 | tf_op jit(solution)/shard_map/ppermute | solution.py:25
  109.1 6.4 %collective-permute-start.8 = (bf16[32,4,128]{2,1,0:T(4,128)(2,1)S(1)}, bf16[32,4,128]{2,1,0:T(4,128)(2,1)S(1)}, u32[]{:S(2)}, u32[]{:S(2)}) collective-permute-start(bf16[32,4,128]{2,1,0:T(4,128)(2,1)S(1)} %get-tuple-element.120), channel_id=1, source_target_pairs={{0,4},{4,8},{8,12},{12,16},{16,20},{20,24},{24,28},{1,5},{5,9},{9,... | collective-permute-start | bytes 98312 | tf_op jit(solution)/shard_map/ppermute | solution.py:15
  113.9 7.0 %collective-permute-start.9 = (bf16[32,4,128]{2,1,0:T(4,128)(2,1)S(1)}, bf16[32,4,128]{2,1,0:T(4,128)(2,1)S(1)}, u32[]{:S(2)}, u32[]{:S(2)}) collective-permute-start(bf16[32,4,128]{2,1,0:T(4,128)(2,1)S(1)} %get-tuple-element.119), channel_id=1, source_target_pairs={{4,0},{8,4},{12,8},{16,12},{20,16},{24,20},{28,24},{5,1},{9,5},{13... | collective-permute-start | bytes 98312 | tf_op jit(solution)/shard_map/ppermute | solution.py:15
  166.9 6.1 %collective-permute-start.11 = (bf16[32,4,128]{2,1,0:T(4,128)(2,1)S(1)}, bf16[32,4,128]{2,1,0:T(4,128)(2,1)S(1)}, u32[]{:S(2)}, u32[]{:S(2)}) collective-permute-start(bf16[32,4,128]{2,1,0:T(4,128)(2,1)S(1)} %get-tuple-element.126), channel_id=1, source_target_pairs={{4,0},{8,4},{12,8},{16,12},{20,16},{24,20},{28,24},{5,1},{9,5},{13... | collective-permute-start | bytes 98312 | tf_op jit(solution)/shard_map/ppermute | solution.py:26
  168.2 6.4 %collective-permute-start.10 = (bf16[32,4,128]{2,1,0:T(4,128)(2,1)S(1)}, bf16[32,4,128]{2,1,0:T(4,128)(2,1)S(1)}, u32[]{:S(2)}, u32[]{:S(2)}) collective-permute-start(bf16[32,4,128]{2,1,0:T(4,128)(2,1)S(1)} %get-tuple-element.125), channel_id=1, source_target_pairs={{0,4},{4,8},{8,12},{12,16},{16,20},{20,24},{24,28},{1,5},{5,9},{9,... | collective-permute-start | bytes 98312 | tf_op jit(solution)/shard_map/ppermute | solution.py:25
  181.7 13.3 %copy-start.2 = (f32[32,16,128]{2,1,0:T(8,128)S(1)}, f32[32,16,128]{2,1,0:T(8,128)}, u32[]{:S(2)}) copy-start(f32[32,16,128]{2,1,0:T(8,128)} %get-tuple-element.111) | copy-start | bytes 786436
  182.3 59.2 %copy-start.1 = (f32[32,16,128]{2,1,0:T(8,128)S(1)}, f32[32,16,128]{2,1,0:T(8,128)}, u32[]{:S(2)}) copy-start(f32[32,16,128]{2,1,0:T(8,128)} %copy-done) | copy-start | bytes 786436
  182.3 59.2 %copy-start.3 = (f32[32,16,128]{2,1,0:T(8,128)S(1)}, f32[32,16,128]{2,1,0:T(8,128)}, u32[]{:S(2)}) copy-start(f32[32,16,128]{2,1,0:T(8,128)} %get-tuple-element.112) | copy-start | bytes 786436
  183.1 6.4 %collective-permute-start.12 = (bf16[32,4,128]{2,1,0:T(4,128)(2,1)S(1)}, bf16[32,4,128]{2,1,0:T(4,128)(2,1)S(1)}, u32[]{:S(2)}, u32[]{:S(2)}) collective-permute-start(bf16[32,4,128]{2,1,0:T(4,128)(2,1)S(1)} %get-tuple-element.118), channel_id=1, source_target_pairs={{0,4},{4,8},{8,12},{12,16},{16,20},{20,24},{24,28},{1,5},{5,9},{9,... | collective-permute-start | bytes 98312 | tf_op jit(solution)/shard_map/ppermute | solution.py:15
  187.9 7.0 %collective-permute-start.13 = (bf16[32,4,128]{2,1,0:T(4,128)(2,1)S(1)}, bf16[32,4,128]{2,1,0:T(4,128)(2,1)S(1)}, u32[]{:S(2)}, u32[]{:S(2)}) collective-permute-start(bf16[32,4,128]{2,1,0:T(4,128)(2,1)S(1)} %get-tuple-element.117), channel_id=1, source_target_pairs={{4,0},{8,4},{12,8},{16,12},{20,16},{24,20},{28,24},{5,1},{9,5},{13... | collective-permute-start | bytes 98312 | tf_op jit(solution)/shard_map/ppermute | solution.py:15
where the time goes:
time: 244 us; the launch traced here: 243 us
  blocking collectives  124 us (51%)
  starting transfers between devices  43.2 us (18%)
  matrix products  29.9 us (12%)
  waiting for transfers between devices  26 us (11%)
  between operations  11.3 us (5%)
  other arithmetic  7.49 us (3%)
    psum x3, blocking collectives, paired(): lax.psum((local_inner(vector, vector), local_inner(vector, applied)), ('t...  124 us
    ppermute x8, starting transfers between devices, from_behind(): return lax.ppermute(value, axis, pairs)  24.5 us
    dot_general x4, matrix products, adjoint_image(): jnp.einsum('cwgf,cgrsf->cwgrs', image16, kernels, preferred_element_type=...  22 us
    ppermute x8, waiting for transfers between devices, from_behind(): return lax.ppermute(value, axis, pairs)  21.5 us
    ppermute x3, starting transfers between devices, extended(): before = lax.ppermute(last, axis, up)  14.8 us
  transfers between devices with their start and end apart: 14, of which 11 were waited for; matrix products, arithmetic and copies ran while one was open for 0% of the time, Pallas kernels for 0%

commit v1 on v0

--- a/solution.py
+++ b/solution.py
@@ -96,7 +96,7 @@
 
     def paired(vector, applied):
         return lax.psum(
-            (local_inner(vector, vector), local_inner(vector, applied)), ("tile", "wave")
+            lax.psum((local_inner(vector, vector), local_inner(vector, applied)), "wave"), "tile"
         )
 
     applied = operate(residual)

time: 244 us -> 196 us (0.80)
  blocking collectives: 124 us -> 80.1 us
    psum x3 -> x6, blocking collectives: 124 us -> 80.1 us  [the longest x3 61.2 us: paired(): lax.psum(lax.psum((local_inner(vector, vector), local_inner(vector, appli...]
where the time goes in v1:
time: 196 us; the launch traced here: 195 us
  blocking collectives  80.1 us (41%)
  starting transfers between devices  41.4 us (21%)
  matrix products  29.9 us (15%)
  waiting for transfers between devices  23.6 us (12%)
  between operations  12 us (6%)
  other arithmetic  7.54 us (4%)
    psum x3, blocking collectives, paired(): lax.psum(lax.psum((local_inner(vector, vector), local_inner(vector, appli...  61.2 us
    ppermute x8, starting transfers between devices, from_behind(): return lax.ppermute(value, axis, pairs)  23.3 us
    dot_general x4, matrix products, adjoint_image(): jnp.einsum('cwgf,cgrsf->cwgrs', image16, kernels, preferred_element_type=...  22 us
    ppermute x8, waiting for transfers between devices, from_behind(): return lax.ppermute(value, axis, pairs)  19.1 us
    psum x3, blocking collectives, paired(): lax.psum((local_inner(vector, vector), local_inner(vector, applied)), 'wa...  18.9 us
    ppermute x3, starting transfers between devices, extended(): before = lax.ppermute(last, axis, up)  14.3 us
    ppermute x3, waiting for transfers between devices, extended(): before = lax.ppermute(last, axis, up)  4.51 us
  transfers between devices with their start and end apart: 14, of which 11 were waited for; matrix products, arithmetic and copies ran while one was open for 0% of the time, Pallas kernels for 0%

profile of v1, /device:TPU:0, one launch (start us, length us, event | category | flops | bytes accessed | tf_op | source)
XLA Modules:
  0.0 195.2 jit_solution(14319018164506953052)
XLA Ops:
  1.3 1.0 multiply_bitcast_fusion
  2.3 3.7 %fusion.12 = f32[32,32,4,128]{3,1,2,0:T(8,128)S(1)} fusion(bf16[1,32,4,128,128]{4,3,2,1,0:T(8,128)(2,1)} %param.21, bf16[32,32,128,1]{2,1,0,3:T(8,128)(2,1)S(1)} %multiply_bitcast_fusion), kind=kOutput, calls=%fused_computation.12 | convolution fusion | flops 134217728 | bytes 6553600 | tf_op jit(solution)/shard_map/cwgf,cgrsf->cwgrs/dot_general | solution.py:48
  7.0 0.7 convolution_bitcast_fusion.6
  7.7 0.7 fusion.153
  8.4 4.9 %collective-permute-start = (bf16[32,4,128]{2,1,0:T(4,128)(2,1)S(1)}, bf16[32,4,128]{2,1,0:T(4,128)(2,1)S(1)}, u32[]{:S(2)}, u32[]{:S(2)}) collective-permute-start(bf16[32,4,128]{2,1,0:T(4,128)(2,1)S(1)} %get-tuple-element.130), channel_id=1, source_target_pairs={{0,4},{4,8},{8,12},{12,16},{16,20},{20,24},{24,28},{1,5},{5,9},{9,... | collective-permute-start | bytes 98312 | tf_op jit(solution)/shard_map/ppermute | solution.py:15
  13.3 1.3 collective-permute-start.1
  14.9 4.2 %collective-permute-done.1 = bf16[32,4,128]{2,1,0:T(4,128)(2,1)S(1)} collective-permute-done((bf16[32,4,128]{2,1,0:T(4,128)(2,1)S(1)}, bf16[32,4,128]{2,1,0:T(4,128)(2,1)S(1)}, u32[]{:S(2)}, u32[]{:S(2)}) %collective-permute-start.1) | collective-permute-done | bytes 32800 | tf_op jit(solution)/shard_map/ppermute | solution.py:15
  19.2 1.3 collective-permute-start.3
  20.5 5.0 %collective-permute-start.2 = (bf16[32,4,128]{2,1,0:T(4,128)(2,1)S(1)}, bf16[32,4,128]{2,1,0:T(4,128)(2,1)S(1)}, u32[]{:S(2)}, u32[]{:S(2)}) collective-permute-start(bf16[32,4,128]{2,1,0:T(4,128)(2,1)S(1)} %get-tuple-element.135), channel_id=1, source_target_pairs={{0,4},{4,8},{8,12},{12,16},{16,20},{20,24},{24,28},{1,5},{5,9},{9,... | collective-permute-start | bytes 98312 | tf_op jit(solution)/shard_map/ppermute | solution.py:25
  25.6 1.6 collective-permute-done.2
  27.1 0.5 fusion.18
  27.6 6.0 %fusion.8 = f32[32,32,4,128]{3,1,2,0:T(8,128)S(1)} fusion(bf16[1,32,4,128,128]{4,3,2,1,0:T(8,128)(2,1)} %param.21, bf16[32,32,4,128]{3,1,2,0:T(8,128)(2,1)S(1)} %fusion.18, f32[32]{0:T(128)S(1)} %compare_convert_fusion), kind=kOutput, calls=%fused_computation.8 | convolution fusion | flops 268697600 | bytes 7340160 | tf_op jit(solution)/shard_map/cwgf,cgrsf->cwgrs/dot_general | solution.py:48
  34.2 0.7 convolution_bitcast_fusion.4
  34.8 0.7 fusion.154
  35.6 4.8 %collective-permute-start.4 = (bf16[32,4,128]{2,1,0:T(4,128)(2,1)S(1)}, bf16[32,4,128]{2,1,0:T(4,128)(2,1)S(1)}, u32[]{:S(2)}, u32[]{:S(2)}) collective-permute-start(bf16[32,4,128]{2,1,0:T(4,128)(2,1)S(1)} %get-tuple-element.128), channel_id=1, source_target_pairs={{0,4},{4,8},{8,12},{12,16},{16,20},{20,24},{24,28},{1,5},{5,9},{9,... | collective-permute-start | bytes 98312 | tf_op jit(solution)/shard_map/ppermute | solution.py:15
  40.4 1.3 collective-permute-start.5
  42.0 5.4 %collective-permute-done.5 = bf16[32,4,128]{2,1,0:T(4,128)(2,1)S(1)} collective-permute-done((bf16[32,4,128]{2,1,0:T(4,128)(2,1)S(1)}, bf16[32,4,128]{2,1,0:T(4,128)(2,1)S(1)}, u32[]{:S(2)}, u32[]{:S(2)}) %collective-permute-start.5) | collective-permute-done | bytes 32800 | tf_op jit(solution)/shard_map/ppermute | solution.py:15
  47.5 0.7 multiply_reduce_fusion.4
  48.2 6.3 %all-reduce.5 = (f32[]{:T(128)}, f32[]{:T(128)}) all-reduce(f32[]{:T(128)} %get-tuple-element.103, f32[]{:T(128)} %get-tuple-element.102), channel_id=1, replica_groups=mesh['tile'=8,'wave'=4] {'wave'}, use_global_device_ids=true, to_apply=%region_1.0 | all-reduce | flops 2 | bytes 16 | tf_op jit(solution)/shard_map/psum | solution.py:99
  54.4 20.9 %all-reduce.2 = (f32[]{:T(128)}, f32[]{:T(128)}) all-reduce(f32[]{:T(128)} %get-tuple-element.114, f32[]{:T(128)} %get-tuple-element.115), channel_id=1, replica_groups=mesh['tile'=8,'wave'=4] {'tile'}, use_global_device_ids=true, to_apply=%region_2.0 | all-reduce | flops 2 | bytes 16 | tf_op jit(solution)/shard_map/psum | solution.py:98
  76.8 1.3 collective-permute-start.7
  78.1 4.7 %collective-permute-start.6 = (bf16[32,4,128]{2,1,0:T(4,128)(2,1)S(1)}, bf16[32,4,128]{2,1,0:T(4,128)(2,1)S(1)}, u32[]{:S(2)}, u32[]{:S(2)}) collective-permute-start(bf16[32,4,128]{2,1,0:T(4,128)(2,1)S(1)} %get-tuple-element.133), channel_id=1, source_target_pairs={{0,4},{4,8},{8,12},{12,16},{16,20},{20,24},{24,28},{1,5},{5,9},{9,... | collective-permute-start | bytes 98312 | tf_op jit(solution)/shard_map/ppermute | solution.py:25
  82.8 1.4 collective-permute-done.6
  84.2 1.5 fusion.19
  85.6 6.3 %fusion.4 = f32[32,32,4,128]{3,1,2,0:T(8,128)S(1)} fusion(bf16[1,32,4,128,128]{4,3,2,1,0:T(8,128)(2,1)} %param.21, bf16[32,32,4,128]{3,1,2,0:T(8,128)(2,1)} %fusion.19, f32[32]{0:T(128)S(1)} %compare_convert_fusion), kind=kOutput, calls=%fused_computation.4 | convolution fusion | flops 268697600 | bytes 7340160 | tf_op jit(solution)/shard_map/cwgf,cgrsf->cwgrs/dot_general | solution.py:48
  92.5 0.7 convolution_bitcast_fusion.2
  93.2 0.7 fusion.155
  93.9 4.2 %collective-permute-start.8 = (bf16[32,4,128]{2,1,0:T(4,128)(2,1)S(1)}, bf16[32,4,128]{2,1,0:T(4,128)(2,1)S(1)}, u32[]{:S(2)}, u32[]{:S(2)}) collective-permute-start(bf16[32,4,128]{2,1,0:T(4,128)(2,1)S(1)} %get-tuple-element.126), channel_id=1, source_target_pairs={{0,4},{4,8},{8,12},{12,16},{16,20},{20,24},{24,28},{1,5},{5,9},{9,... | collective-permute-start | bytes 98312 | tf_op jit(solution)/shard_map/ppermute | solution.py:15
  98.1 1.3 collective-permute-start.9
  99.7 4.2 %collective-permute-done.9 = bf16[32,4,128]{2,1,0:T(4,128)(2,1)S(1)} collective-permute-done((bf16[32,4,128]{2,1,0:T(4,128)(2,1)S(1)}, bf16[32,4,128]{2,1,0:T(4,128)(2,1)S(1)}, u32[]{:S(2)}, u32[]{:S(2)}) %collective-permute-start.9) | collective-permute-done | bytes 32800 | tf_op jit(solution)/shard_map/ppermute | solution.py:15
  104.0 0.7 multiply_reduce_fusion.2
  104.7 6.3 %all-reduce.4 = (f32[]{:T(128)}, f32[]{:T(128)}) all-reduce(f32[]{:T(128)} %get-tuple-element.101, f32[]{:T(128)} %get-tuple-element.100), channel_id=1, replica_groups=mesh['tile'=8,'wave'=4] {'wave'}, use_global_device_ids=true, to_apply=%region_7.0 | all-reduce | flops 2 | bytes 16 | tf_op jit(solution)/shard_map/psum | solution.py:99
  111.1 19.6 %all-reduce.1 = (f32[]{:T(128)}, f32[]{:T(128)}) all-reduce(f32[]{:T(128)} %get-tuple-element.112, f32[]{:T(128)} %get-tuple-element.113), channel_id=1, replica_groups=mesh['tile'=8,'wave'=4] {'tile'}, use_global_device_ids=true, to_apply=%region_8.0 | all-reduce | flops 2 | bytes 16 | tf_op jit(solution)/shard_map/psum | solution.py:98
  135.4 0.9 fusion.144
  136.3 1.3 collective-permute-start.11
  137.7 4.5 %collective-permute-start.10 = (bf16[32,4,128]{2,1,0:T(4,128)(2,1)S(1)}, bf16[32,4,128]{2,1,0:T(4,128)(2,1)S(1)}, u32[]{:S(2)}, u32[]{:S(2)}) collective-permute-start(bf16[32,4,128]{2,1,0:T(4,128)(2,1)S(1)} %get-tuple-element.131), channel_id=1, source_target_pairs={{0,4},{4,8},{8,12},{12,16},{16,20},{20,24},{24,28},{1,5},{5,9},{9,... | collective-permute-start | bytes 98312 | tf_op jit(solution)/shard_map/ppermute | solution.py:25
  142.2 1.6 collective-permute-done.10
  143.8 0.5 fusion.20
  144.3 6.0 %fusion = f32[32,32,4,128]{3,1,2,0:T(8,128)S(1)} fusion(bf16[1,32,4,128,128]{4,3,2,1,0:T(8,128)(2,1)} %param.21, bf16[32,32,4,128]{3,1,2,0:T(8,128)(2,1)S(1)} %fusion.20, f32[32]{0:T(128)S(1)} %compare_convert_fusion), kind=kOutput, calls=%fused_computation | convolution fusion | flops 268697600 | bytes 7340160 | tf_op jit(solution)/shard_map/cwgf,cgrsf->cwgrs/dot_general | solution.py:48
  150.8 0.7 convolution_bitcast_fusion
  151.5 0.7 fusion.156
  152.3 4.2 %collective-permute-start.12 = (bf16[32,4,128]{2,1,0:T(4,128)(2,1)S(1)}, bf16[32,4,128]{2,1,0:T(4,128)(2,1)S(1)}, u32[]{:S(2)}, u32[]{:S(2)}) collective-permute-start(bf16[32,4,128]{2,1,0:T(4,128)(2,1)S(1)} %get-tuple-element.124), channel_id=1, source_target_pairs={{0,4},{4,8},{8,12},{12,16},{16,20},{20,24},{24,28},{1,5},{5,9},{9,... | collective-permute-start | bytes 98312 | tf_op jit(solution)/shard_map/ppermute | solution.py:15
  156.5 1.3 collective-permute-start.13
  158.1 4.2 %collective-permute-done.13 = bf16[32,4,128]{2,1,0:T(4,128)(2,1)S(1)} collective-permute-done((bf16[32,4,128]{2,1,0:T(4,128)(2,1)S(1)}, bf16[32,4,128]{2,1,0:T(4,128)(2,1)S(1)}, u32[]{:S(2)}, u32[]{:S(2)}) %collective-permute-start.13) | collective-permute-done | bytes 32800 | tf_op jit(solution)/shard_map/ppermute | solution.py:15
  162.4 0.8 multiply_reduce_fusion
  163.1 6.3 %all-reduce.3 = (f32[]{:T(128)}, f32[]{:T(128)}) all-reduce(f32[]{:T(128)} %get-tuple-element.99, f32[]{:T(128)} %get-tuple-element.98), channel_id=1, replica_groups=mesh['tile'=8,'wave'=4] {'wave'}, use_global_device_ids=true, to_apply=%region_13.0 | all-reduce | flops 2 | bytes 16 | tf_op jit(solution)/shard_map/psum | solution.py:99
  169.4 20.7 %all-reduce = (f32[]{:T(128)}, f32[]{:T(128)}) all-reduce(f32[]{:T(128)} %get-tuple-element.110, f32[]{:T(128)} %get-tuple-element.111), channel_id=1, replica_groups=mesh['tile'=8,'wave'=4] {'tile'}, use_global_device_ids=true, to_apply=%region_14.0 | all-reduce | flops 2 | bytes 16 | tf_op jit(solution)/shard_map/psum | solution.py:98
  194.3 0.9 multiply_subtract_fusion
  (49 shorter events, 4.2 us)
Async XLA Ops:
  6.4 0.7 copy-start.4
  8.4 6.5 %collective-permute-start = (bf16[32,4,128]{2,1,0:T(4,128)(2,1)S(1)}, bf16[32,4,128]{2,1,0:T(4,128)(2,1)S(1)}, u32[]{:S(2)}, u32[]{:S(2)}) collective-permute-start(bf16[32,4,128]{2,1,0:T(4,128)(2,1)S(1)} %get-tuple-element.130), channel_id=1, source_target_pairs={{0,4},{4,8},{8,12},{12,16},{16,20},{20,24},{24,28},{1,5},{5,9},{9,... | collective-permute-start | bytes 98312 | tf_op jit(solution)/shard_map/ppermute | solution.py:15
  13.3 5.8 %collective-permute-start.1 = (bf16[32,4,128]{2,1,0:T(4,128)(2,1)S(1)}, bf16[32,4,128]{2,1,0:T(4,128)(2,1)S(1)}, u32[]{:S(2)}, u32[]{:S(2)}) collective-permute-start(bf16[32,4,128]{2,1,0:T(4,128)(2,1)S(1)} %get-tuple-element.129), channel_id=1, source_target_pairs={{4,0},{8,4},{12,8},{16,12},{20,16},{24,20},{28,24},{5,1},{9,5},{13... | collective-permute-start | bytes 98312 | tf_op jit(solution)/shard_map/ppermute | solution.py:15
  19.2 6.3 %collective-permute-start.3 = (bf16[32,4,128]{2,1,0:T(4,128)(2,1)S(1)}, bf16[32,4,128]{2,1,0:T(4,128)(2,1)S(1)}, u32[]{:S(2)}, u32[]{:S(2)}) collective-permute-start(bf16[32,4,128]{2,1,0:T(4,128)(2,1)S(1)} %get-tuple-element.136), channel_id=1, source_target_pairs={{4,0},{8,4},{12,8},{16,12},{20,16},{24,20},{28,24},{5,1},{9,5},{13... | collective-permute-start | bytes 98312 | tf_op jit(solution)/shard_map/ppermute | solution.py:26
  20.5 6.6 %collective-permute-start.2 = (bf16[32,4,128]{2,1,0:T(4,128)(2,1)S(1)}, bf16[32,4,128]{2,1,0:T(4,128)(2,1)S(1)}, u32[]{:S(2)}, u32[]{:S(2)}) collective-permute-start(bf16[32,4,128]{2,1,0:T(4,128)(2,1)S(1)} %get-tuple-element.135), channel_id=1, source_target_pairs={{0,4},{4,8},{8,12},{12,16},{16,20},{20,24},{24,28},{1,5},{5,9},{9,... | collective-permute-start | bytes 98312 | tf_op jit(solution)/shard_map/ppermute | solution.py:25
  35.6 6.4 %collective-permute-start.4 = (bf16[32,4,128]{2,1,0:T(4,128)(2,1)S(1)}, bf16[32,4,128]{2,1,0:T(4,128)(2,1)S(1)}, u32[]{:S(2)}, u32[]{:S(2)}) collective-permute-start(bf16[32,4,128]{2,1,0:T(4,128)(2,1)S(1)} %get-tuple-element.128), channel_id=1, source_target_pairs={{0,4},{4,8},{8,12},{12,16},{16,20},{20,24},{24,28},{1,5},{5,9},{9,... | collective-permute-start | bytes 98312 | tf_op jit(solution)/shard_map/ppermute | solution.py:15
  40.4 7.0 %collective-permute-start.5 = (bf16[32,4,128]{2,1,0:T(4,128)(2,1)S(1)}, bf16[32,4,128]{2,1,0:T(4,128)(2,1)S(1)}, u32[]{:S(2)}, u32[]{:S(2)}) collective-permute-start(bf16[32,4,128]{2,1,0:T(4,128)(2,1)S(1)} %get-tuple-element.127), channel_id=1, source_target_pairs={{4,0},{8,4},{12,8},{16,12},{20,16},{24,20},{28,24},{5,1},{9,5},{13... | collective-permute-start | bytes 98312 | tf_op jit(solution)/shard_map/ppermute | solution.py:15
  76.7 58.7 %copy-start = (f32[32,16,128]{2,1,0:T(8,128)}, f32[32,16,128]{2,1,0:T(8,128)S(1)}, u32[]{:S(2)}) copy-start(f32[32,16,128]{2,1,0:T(8,128)S(1)} %get-tuple-element.120) | copy-start | bytes 786436
  76.8 6.0 %collective-permute-start.7 = (bf16[32,4,128]{2,1,0:T(4,128)(2,1)S(1)}, bf16[32,4,128]{2,1,0:T(4,128)(2,1)S(1)}, u32[]{:S(2)}, u32[]{:S(2)}) collective-permute-start(bf16[32,4,128]{2,1,0:T(4,128)(2,1)S(1)} %get-tuple-element.134), channel_id=1, source_target_pairs={{4,0},{8,4},{12,8},{16,12},{20,16},{24,20},{28,24},{5,1},{9,5},{13... | collective-permute-start | bytes 98312 | tf_op jit(solution)/shard_map/ppermute | solution.py:26
  78.1 6.1 %collective-permute-start.6 = (bf16[32,4,128]{2,1,0:T(4,128)(2,1)S(1)}, bf16[32,4,128]{2,1,0:T(4,128)(2,1)S(1)}, u32[]{:S(2)}, u32[]{:S(2)}) collective-permute-start(bf16[32,4,128]{2,1,0:T(4,128)(2,1)S(1)} %get-tuple-element.133), channel_id=1, source_target_pairs={{0,4},{4,8},{8,12},{12,16},{16,20},{20,24},{24,28},{1,5},{5,9},{9,... | collective-permute-start | bytes 98312 | tf_op jit(solution)/shard_map/ppermute | solution.py:25
  93.9 5.8 %collective-permute-start.8 = (bf16[32,4,128]{2,1,0:T(4,128)(2,1)S(1)}, bf16[32,4,128]{2,1,0:T(4,128)(2,1)S(1)}, u32[]{:S(2)}, u32[]{:S(2)}) collective-permute-start(bf16[32,4,128]{2,1,0:T(4,128)(2,1)S(1)} %get-tuple-element.126), channel_id=1, source_target_pairs={{0,4},{4,8},{8,12},{12,16},{16,20},{20,24},{24,28},{1,5},{5,9},{9,... | collective-permute-start | bytes 98312 | tf_op jit(solution)/shard_map/ppermute | solution.py:15
  98.1 5.8 %collective-permute-start.9 = (bf16[32,4,128]{2,1,0:T(4,128)(2,1)S(1)}, bf16[32,4,128]{2,1,0:T(4,128)(2,1)S(1)}, u32[]{:S(2)}, u32[]{:S(2)}) collective-permute-start(bf16[32,4,128]{2,1,0:T(4,128)(2,1)S(1)} %get-tuple-element.125), channel_id=1, source_target_pairs={{4,0},{8,4},{12,8},{16,12},{20,16},{24,20},{28,24},{5,1},{9,5},{13... | collective-permute-start | bytes 98312 | tf_op jit(solution)/shard_map/ppermute | solution.py:15
  136.3 5.9 %collective-permute-start.11 = (bf16[32,4,128]{2,1,0:T(4,128)(2,1)S(1)}, bf16[32,4,128]{2,1,0:T(4,128)(2,1)S(1)}, u32[]{:S(2)}, u32[]{:S(2)}) collective-permute-start(bf16[32,4,128]{2,1,0:T(4,128)(2,1)S(1)} %get-tuple-element.132), channel_id=1, source_target_pairs={{4,0},{8,4},{12,8},{16,12},{20,16},{24,20},{28,24},{5,1},{9,5},{13... | collective-permute-start | bytes 98312 | tf_op jit(solution)/shard_map/ppermute | solution.py:26
  137.7 6.1 %collective-permute-start.10 = (bf16[32,4,128]{2,1,0:T(4,128)(2,1)S(1)}, bf16[32,4,128]{2,1,0:T(4,128)(2,1)S(1)}, u32[]{:S(2)}, u32[]{:S(2)}) collective-permute-start(bf16[32,4,128]{2,1,0:T(4,128)(2,1)S(1)} %get-tuple-element.131), channel_id=1, source_target_pairs={{0,4},{4,8},{8,12},{12,16},{16,20},{20,24},{24,28},{1,5},{5,9},{9,... | collective-permute-start | bytes 98312 | tf_op jit(solution)/shard_map/ppermute | solution.py:25
  150.8 11.5 %copy-start.2 = (f32[32,16,128]{2,1,0:T(8,128)S(1)}, f32[32,16,128]{2,1,0:T(8,128)}, u32[]{:S(2)}) copy-start(f32[32,16,128]{2,1,0:T(8,128)} %get-tuple-element.117) | copy-start | bytes 786436
  151.5 42.8 %copy-start.1 = (f32[32,16,128]{2,1,0:T(8,128)S(1)}, f32[32,16,128]{2,1,0:T(8,128)}, u32[]{:S(2)}) copy-start(f32[32,16,128]{2,1,0:T(8,128)} %copy-done) | copy-start | bytes 786436
  151.5 42.8 %copy-start.3 = (f32[32,16,128]{2,1,0:T(8,128)S(1)}, f32[32,16,128]{2,1,0:T(8,128)}, u32[]{:S(2)}) copy-start(f32[32,16,128]{2,1,0:T(8,128)} %get-tuple-element.118) | copy-start | bytes 786436
  152.3 5.8 %collective-permute-start.12 = (bf16[32,4,128]{2,1,0:T(4,128)(2,1)S(1)}, bf16[32,4,128]{2,1,0:T(4,128)(2,1)S(1)}, u32[]{:S(2)}, u32[]{:S(2)}) collective-permute-start(bf16[32,4,128]{2,1,0:T(4,128)(2,1)S(1)} %get-tuple-element.124), channel_id=1, source_target_pairs={{0,4},{4,8},{8,12},{12,16},{16,20},{20,24},{24,28},{1,5},{5,9},{9,... | collective-permute-start | bytes 98312 | tf_op jit(solution)/shard_map/ppermute | solution.py:15
  156.5 5.8 %collective-permute-start.13 = (bf16[32,4,128]{2,1,0:T(4,128)(2,1)S(1)}, bf16[32,4,128]{2,1,0:T(4,128)(2,1)S(1)}, u32[]{:S(2)}, u32[]{:S(2)}) collective-permute-start(bf16[32,4,128]{2,1,0:T(4,128)(2,1)S(1)} %get-tuple-element.123), channel_id=1, source_target_pairs={{4,0},{8,4},{12,8},{16,12},{20,16},{24,20},{28,24},{5,1},{9,5},{13... | collective-permute-start | bytes 98312 | tf_op jit(solution)/shard_map/ppermute | solution.py:15
